TPU v7x, 32 devices: a whole 2x2x4 slice. The times are simulated.
32 devices in a mesh: grp: 2 (over y), inp: 4 (over z), tm: 2 (over x), pol: 2 (over core).
Axes of the slice: x: 2, y: 2, z: 4, core: 2. Of those that a mesh axis runs over, the one named last changes fastest.
Arguments:
- samples: bfloat16 [512, 64, 4096], P(('grp', 'inp'), ('tm', 'pol')), parts along dimension 0, may hold values from -6 to 6
- coefficients: float32 [16, 4096], replicated, may hold values from -1.5 to 1.5
Outputs:
- visibilities: float32 [4096, 256, 256], P(('grp', 'inp', 'tm', 'pol')), parts along dimension 0
There are 2 independent parts, one for each index of `grp`. A program takes and returns all parts, laid end to end along the dimension named above; an argument that names none is the same for every part. Nothing has to cross between parts.
All inputs are finite; a program needn't handle non-finite values.
Results may differ from a plain program's by a relative error of at most 0.0034.
Values may be sent and summed in bfloat16 or wider, within the bound.
No kernel may reach another device: no remote copies, remote signals or barrier semaphores. Data moves between devices by JAX's collectives and lax.ppermute only.
A program may use at most 256 MiB of HBM per device.

v0:
```python
import math
import jax
import jax.numpy as jnp
from jax import lax
from jax.sharding import PartitionSpec as P


def from_behind(block, axis, distance):
    devices = range(lax.axis_size(axis))
    route = [(i - distance, i) for i in devices if i - distance in devices]
    return lax.ppermute(block, axis, route)


def correlate(real_part, imag_part, total_frames):
    joined = jnp.concatenate([real_part, imag_part], axis=2)
    turned = jnp.concatenate([imag_part, -real_part], axis=2)
    stacked = jnp.concatenate([joined, turned], axis=1)
    product = jnp.einsum("cif,cjf->cij", stacked, joined, preferred_element_type=jnp.float32)
    width = real_part.shape[1]
    row_index = lax.broadcasted_iota(jnp.int32, (width, width), 0)
    col_index = lax.broadcasted_iota(jnp.int32, (width, width), 1)
    packed = jnp.where(row_index <= col_index, product[:, :width], product[:, width:])
    return packed * (1.0 / total_frames)


def filter_frames(block, coefficients, taps):
    frame_count = block.shape[1] - taps + 1
    total = jnp.zeros((block.shape[0], frame_count, block.shape[2]), jnp.float32)
    for tap_index in range(taps):
        total = total + coefficients[tap_index] * block[
            :, tap_index : tap_index + frame_count
        ].astype(jnp.float32)
    return total


def angles(first_idx, second_idx, period):
    product = first_idx[:, None] * second_idx[None, :] % period
    return product.astype(jnp.float32) * (2.0 * math.pi / period)


def transform(filtered):
    row_total, length = filtered.shape
    inner_len = 2 ** ((length.bit_length() - 1) // 2)
    outer_len = length // inner_len
    blocks = filtered.reshape(row_total, inner_len, outer_len)
    inner_idx = jnp.arange(inner_len, dtype=jnp.int32)
    outer_idx = jnp.arange(outer_len, dtype=jnp.int32)
    half_idx = jnp.arange(outer_len // 2, dtype=jnp.int32)
    angle_one = angles(inner_idx, inner_idx, inner_len)
    table_one = jnp.concatenate([jnp.cos(angle_one), -jnp.sin(angle_one)], axis=1)
    section_one = jnp.einsum("rab,ak->rbk", blocks, table_one, precision=lax.Precision.HIGHEST)
    first_re = section_one[..., :inner_len]
    first_im = section_one[..., inner_len:]
    angle_twist = angles(outer_idx, inner_idx, length)
    twist_cos = jnp.cos(angle_twist)
    twist_sin = jnp.sin(angle_twist)
    turned_re = first_re * twist_cos + first_im * twist_sin
    turned_im = first_im * twist_cos - first_re * twist_sin
    angle_two = angles(outer_idx, half_idx, outer_len)
    table_cos = jnp.cos(angle_two)
    table_sin = jnp.sin(angle_two)
    highest = lax.Precision.HIGHEST
    out_re = jnp.einsum("rbk,bq->qkr", turned_re, table_cos, precision=highest) + jnp.einsum(
        "rbk,bq->qkr", turned_im, table_sin, precision=highest
    )
    out_im = jnp.einsum("rbk,bq->qkr", turned_im, table_cos, precision=highest) - jnp.einsum(
        "rbk,bq->qkr", turned_re, table_sin, precision=highest
    )
    scale_factor = 1.0 / math.sqrt(length)
    return jnp.stack([out_re, out_im]).reshape(2, length // 2, row_total) * scale_factor


def per_device(samples, coefficients):
    in_dev, frame_count, length = samples.shape
    taps = coefficients.shape[0]
    channels = length // 2
    history = from_behind(samples[:, frame_count - taps + 1 :, :], ("tm", "pol"), 1)
    extended = jnp.concatenate([history, samples], axis=1)
    group_size = math.gcd(in_dev, 4)
    spectra_buf = jnp.zeros((2, channels, in_dev, frame_count), jnp.bfloat16)

    def one_group(group_index, buffer_now):
        block = lax.dynamic_slice_in_dim(extended, group_index * group_size, group_size, 0)
        filtered = filter_frames(block, coefficients, taps).reshape(
            group_size * frame_count, length
        )
        spectra_grp = (
            transform(filtered).reshape(2, channels, group_size, frame_count).astype(jnp.bfloat16)
        )
        return lax.dynamic_update_slice_in_dim(buffer_now, spectra_grp, group_index * group_size, 2)

    local_spec = lax.fori_loop(0, in_dev // group_size, one_group, spectra_buf)
    n_inputs = lax.axis_size("inp")
    n_blocks = lax.axis_size("tm")
    n_halves = lax.axis_size("pol")
    total_frames = frame_count * n_blocks * n_halves
    arrived = lax.all_to_all(
        local_spec[None], ("inp", "tm", "pol"), split_axis=2, concat_axis=0, tiled=True
    )
    width = arrived.shape[2]
    arrived = arrived.reshape(n_inputs, n_blocks * n_halves, 2, width, in_dev, frame_count)
    arrived = jnp.transpose(arrived, (2, 3, 0, 4, 1, 5)).reshape(
        2, width, n_inputs * in_dev, n_blocks * n_halves * frame_count
    )
    return correlate(arrived[0], arrived[1], total_frames)


def solution(mesh):
    placed = (P(("grp", "inp"), ("tm", "pol"), None), P())
    return jax.shard_map(
        per_device,
        mesh=mesh,
        in_specs=placed,
        out_specs=P(("grp", "inp", "tm", "pol"), None, None),
        check_vma=False,
    )
```

profile of v0, /device:TPU:11, one launch (start us, length us, event | category | flops | bytes accessed | tf_op | source)
XLA Modules:
  0.0 989.7 jit_solution(8066666141013795568)
XLA Ops:
  0.0 10.5 %slice.391 = bf16[64,15,4096]{2,1,0:T(8,128)(2,1)} slice(bf16[64,16,4096]{2,1,0:T(8,128)(2,1)} %param.4), slice={[0:64], [1:16], [0:4096]} | slice | bytes 15728640 | tf_op jit(solution)/shard_map/slice | solution.py:77
  10.5 11.0 %copy.61 = bf16[64,15,4096]{2,0,1:T(8,128)(2,1)} copy(bf16[64,15,4096]{2,1,0:T(8,128)(2,1)} %slice.391) | data formatting | bytes 15728640
  23.3 13.1 %collective-permute-done = bf16[64,15,4096]{2,0,1:T(8,128)(2,1)} collective-permute-done((bf16[64,15,4096]{2,0,1:T(8,128)(2,1)}, bf16[64,15,4096]{2,0,1:T(8,128)(2,1)}, u32[]{:S(2)}, u32[]{:S(2)}) %collective-permute-start) | collective-permute-done | bytes 7864352 | tf_op jit(solution)/shard_map/ppermute | solution.py:11
  36.3 10.8 %copy.45 = bf16[64,15,4096]{2,1,0:T(8,128)(2,1)} copy(bf16[64,15,4096]{2,0,1:T(8,128)(2,1)} %collective-permute-done) | data formatting | bytes 15728640 | tf_op jit(solution)/shard_map/ppermute | solution.py:11
  47.1 14.9 %pad_maximum_fusion = bf16[64,31,4096]{2,1,0:T(8,128)(2,1)} fusion(bf16[64,16,4096]{2,1,0:T(8,128)(2,1)} %param.4, bf16[64,15,4096]{2,1,0:T(8,128)(2,1)} %copy.45), kind=kLoop, calls=%fused_computation.71 | loop fusion | flops 32505856 | bytes 32505856 | tf_op jit(solution)/shard_map/concatenate | solution.py:78
  66.4 447.3 %while.16 = (s32[]{:T(128)}, bf16[2,2048,64,16]{1,3,2,0:T(8,128)(2,1)}, f32[16,4096]{1,0:T(8,128)S(1)}, bf16[64,31,4096]{2,1,0:T(8,128)(2,1)}, s32[]{:T(128)}, /...) while((s32[]{:T(128)}, ...), condition=%wide.region_1.2_spmd, body=%wide.region_0.1_spmd.sunk | while | flops 822063104 | bytes 40468980 | solution.py:92
  67.1 10.2 %multiply_add_fusion.9 = f32[4,16,4096]{2,1,0:T(8,128)S(1)} fusion(bf16[64,31,4096]{2,1,0:T(8,128)(2,1)} %get-tuple-element.280, s32[]{:T(128)S(6)} %select_n.151, s32[]{:T(128)S(6)} %add.431, s32[]{:T(128)S(6)} %add.432, s32[]{:T(128)S(6)} %add.433, s32[]{:T(128)S(6)} %add.434, s32[]{:T(128)S(6)} %add.435, s32[]{:T(128)S(6)} %add.436, s32[]{:T(128)S(6)} %add.437, ...), kind=kLoop, calls=%fused_computation.8.clone.1 | loop fusion | flops 12320768 | bytes 9699392 | tf_op jit(solution)/shard_map/while/body/eval_jaxpr/add | solution.py:30
  79.5 5.0 fusion.97
  95.0 9.7 multiply_add_fusion.9
  106.9 5.0 fusion.97
  122.4 10.7 %multiply_add_fusion.9 = f32[4,16,4096]{2,1,0:T(8,128)S(1)} fusion(bf16[64,31,4096]{2,1,0:T(8,128)(2,1)} %get-tuple-element.280, s32[]{:T(128)S(6)} %select_n.151, s32[]{:T(128)S(6)} %add.431, s32[]{:T(128)S(6)} %add.432, s32[]{:T(128)S(6)} %add.433, s32[]{:T(128)S(6)} %add.434, s32[]{:T(128)S(6)} %add.435, s32[]{:T(128)S(6)} %add.436, s32[]{:T(128)S(6)} %add.437, ...), kind=kLoop, calls=%fused_computation.8.clone.1 | loop fusion | flops 12320768 | bytes 9699392 | tf_op jit(solution)/shard_map/while/body/eval_jaxpr/add | solution.py:30
  135.3 5.0 fusion.97
  150.9 9.9 %multiply_add_fusion.9 = f32[4,16,4096]{2,1,0:T(8,128)S(1)} fusion(bf16[64,31,4096]{2,1,0:T(8,128)(2,1)} %get-tuple-element.280, s32[]{:T(128)S(6)} %select_n.151, s32[]{:T(128)S(6)} %add.431, s32[]{:T(128)S(6)} %add.432, s32[]{:T(128)S(6)} %add.433, s32[]{:T(128)S(6)} %add.434, s32[]{:T(128)S(6)} %add.435, s32[]{:T(128)S(6)} %add.436, s32[]{:T(128)S(6)} %add.437, ...), kind=kLoop, calls=%fused_computation.8.clone.1 | loop fusion | flops 12320768 | bytes 9699392 | tf_op jit(solution)/shard_map/while/body/eval_jaxpr/add | solution.py:30
  163.0 5.0 fusion.97
  178.5 9.5 multiply_add_fusion.9
  190.3 5.0 fusion.97
  205.8 10.1 %multiply_add_fusion.9 = f32[4,16,4096]{2,1,0:T(8,128)S(1)} fusion(bf16[64,31,4096]{2,1,0:T(8,128)(2,1)} %get-tuple-element.280, s32[]{:T(128)S(6)} %select_n.151, s32[]{:T(128)S(6)} %add.431, s32[]{:T(128)S(6)} %add.432, s32[]{:T(128)S(6)} %add.433, s32[]{:T(128)S(6)} %add.434, s32[]{:T(128)S(6)} %add.435, s32[]{:T(128)S(6)} %add.436, s32[]{:T(128)S(6)} %add.437, ...), kind=kLoop, calls=%fused_computation.8.clone.1 | loop fusion | flops 12320768 | bytes 9699392 | tf_op jit(solution)/shard_map/while/body/eval_jaxpr/add | solution.py:30
  218.1 5.0 fusion.97
  233.6 10.9 %multiply_add_fusion.9 = f32[4,16,4096]{2,1,0:T(8,128)S(1)} fusion(bf16[64,31,4096]{2,1,0:T(8,128)(2,1)} %get-tuple-element.280, s32[]{:T(128)S(6)} %select_n.151, s32[]{:T(128)S(6)} %add.431, s32[]{:T(128)S(6)} %add.432, s32[]{:T(128)S(6)} %add.433, s32[]{:T(128)S(6)} %add.434, s32[]{:T(128)S(6)} %add.435, s32[]{:T(128)S(6)} %add.436, s32[]{:T(128)S(6)} %add.437, ...), kind=kLoop, calls=%fused_computation.8.clone.1 | loop fusion | flops 12320768 | bytes 9699392 | tf_op jit(solution)/shard_map/while/body/eval_jaxpr/add | solution.py:30
  262.3 9.6 multiply_add_fusion.9
  274.0 5.0 fusion.97
  289.6 10.2 %multiply_add_fusion.9 = f32[4,16,4096]{2,1,0:T(8,128)S(1)} fusion(bf16[64,31,4096]{2,1,0:T(8,128)(2,1)} %get-tuple-element.280, s32[]{:T(128)S(6)} %select_n.151, s32[]{:T(128)S(6)} %add.431, s32[]{:T(128)S(6)} %add.432, s32[]{:T(128)S(6)} %add.433, s32[]{:T(128)S(6)} %add.434, s32[]{:T(128)S(6)} %add.435, s32[]{:T(128)S(6)} %add.436, s32[]{:T(128)S(6)} %add.437, ...), kind=kLoop, calls=%fused_computation.8.clone.1 | loop fusion | flops 12320768 | bytes 9699392 | tf_op jit(solution)/shard_map/while/body/eval_jaxpr/add | solution.py:30
  317.5 9.8 multiply_add_fusion.9
  329.5 5.0 fusion.97
  345.0 10.2 %multiply_add_fusion.9 = f32[4,16,4096]{2,1,0:T(8,128)S(1)} fusion(bf16[64,31,4096]{2,1,0:T(8,128)(2,1)} %get-tuple-element.280, s32[]{:T(128)S(6)} %select_n.151, s32[]{:T(128)S(6)} %add.431, s32[]{:T(128)S(6)} %add.432, s32[]{:T(128)S(6)} %add.433, s32[]{:T(128)S(6)} %add.434, s32[]{:T(128)S(6)} %add.435, s32[]{:T(128)S(6)} %add.436, s32[]{:T(128)S(6)} %add.437, ...), kind=kLoop, calls=%fused_computation.8.clone.1 | loop fusion | flops 12320768 | bytes 9699392 | tf_op jit(solution)/shard_map/while/body/eval_jaxpr/add | solution.py:30
  357.5 5.0 fusion.97
  373.0 10.8 %multiply_add_fusion.9 = f32[4,16,4096]{2,1,0:T(8,128)S(1)} fusion(bf16[64,31,4096]{2,1,0:T(8,128)(2,1)} %get-tuple-element.280, s32[]{:T(128)S(6)} %select_n.151, s32[]{:T(128)S(6)} %add.431, s32[]{:T(128)S(6)} %add.432, s32[]{:T(128)S(6)} %add.433, s32[]{:T(128)S(6)} %add.434, s32[]{:T(128)S(6)} %add.435, s32[]{:T(128)S(6)} %add.436, s32[]{:T(128)S(6)} %add.437, ...), kind=kLoop, calls=%fused_computation.8.clone.1 | loop fusion | flops 12320768 | bytes 9699392 | tf_op jit(solution)/shard_map/while/body/eval_jaxpr/add | solution.py:30
  401.5 10.7 %multiply_add_fusion.9 = f32[4,16,4096]{2,1,0:T(8,128)S(1)} fusion(bf16[64,31,4096]{2,1,0:T(8,128)(2,1)} %get-tuple-element.280, s32[]{:T(128)S(6)} %select_n.151, s32[]{:T(128)S(6)} %add.431, s32[]{:T(128)S(6)} %add.432, s32[]{:T(128)S(6)} %add.433, s32[]{:T(128)S(6)} %add.434, s32[]{:T(128)S(6)} %add.435, s32[]{:T(128)S(6)} %add.436, s32[]{:T(128)S(6)} %add.437, ...), kind=kLoop, calls=%fused_computation.8.clone.1 | loop fusion | flops 12320768 | bytes 9699392 | tf_op jit(solution)/shard_map/while/body/eval_jaxpr/add | solution.py:30
  414.5 5.0 fusion.97
  430.0 10.3 %multiply_add_fusion.9 = f32[4,16,4096]{2,1,0:T(8,128)S(1)} fusion(bf16[64,31,4096]{2,1,0:T(8,128)(2,1)} %get-tuple-element.280, s32[]{:T(128)S(6)} %select_n.151, s32[]{:T(128)S(6)} %add.431, s32[]{:T(128)S(6)} %add.432, s32[]{:T(128)S(6)} %add.433, s32[]{:T(128)S(6)} %add.434, s32[]{:T(128)S(6)} %add.435, s32[]{:T(128)S(6)} %add.436, s32[]{:T(128)S(6)} %add.437, ...), kind=kLoop, calls=%fused_computation.8.clone.1 | loop fusion | flops 12320768 | bytes 9699392 | tf_op jit(solution)/shard_map/while/body/eval_jaxpr/add | solution.py:30
  458.0 10.4 %multiply_add_fusion.9 = f32[4,16,4096]{2,1,0:T(8,128)S(1)} fusion(bf16[64,31,4096]{2,1,0:T(8,128)(2,1)} %get-tuple-element.280, s32[]{:T(128)S(6)} %select_n.151, s32[]{:T(128)S(6)} %add.431, s32[]{:T(128)S(6)} %add.432, s32[]{:T(128)S(6)} %add.433, s32[]{:T(128)S(6)} %add.434, s32[]{:T(128)S(6)} %add.435, s32[]{:T(128)S(6)} %add.436, s32[]{:T(128)S(6)} %add.437, ...), kind=kLoop, calls=%fused_computation.8.clone.1 | loop fusion | flops 12320768 | bytes 9699392 | tf_op jit(solution)/shard_map/while/body/eval_jaxpr/add | solution.py:30
  486.1 10.1 %multiply_add_fusion.9 = f32[4,16,4096]{2,1,0:T(8,128)S(1)} fusion(bf16[64,31,4096]{2,1,0:T(8,128)(2,1)} %get-tuple-element.280, s32[]{:T(128)S(6)} %select_n.151, s32[]{:T(128)S(6)} %add.431, s32[]{:T(128)S(6)} %add.432, s32[]{:T(128)S(6)} %add.433, s32[]{:T(128)S(6)} %add.434, s32[]{:T(128)S(6)} %add.435, s32[]{:T(128)S(6)} %add.436, s32[]{:T(128)S(6)} %add.437, ...), kind=kLoop, calls=%fused_computation.8.clone.1 | loop fusion | flops 12320768 | bytes 9699392 | tf_op jit(solution)/shard_map/while/body/eval_jaxpr/add | solution.py:30
  498.4 5.0 fusion.97
  513.6 28.6 %copy.46 = bf16[2,2048,64,16]{2,3,0,1:T(8,128)(2,1)} copy(bf16[2,2048,64,16]{1,3,2,0:T(8,128)(2,1)} %get-tuple-element.135) | data formatting | bytes 16777216 | tf_op jit(solution)/shard_map/while | solution.py:92
  542.2 14.5 %bitcast_bitcast_fusion = bf16[2048,1,2,16,64]{4,3,2,1,0:T(8,128)(2,1)} fusion(bf16[2,2048,64,16]{2,3,0,1:T(8,128)(2,1)} %copy.46), kind=kLoop, calls=%fused_computation.87 | loop fusion | bytes 16777216
  556.7 19.6 %reshape.97 = bf16[16,2,131072]{2,1,0:T(2,128)(2,1)} reshape(bf16[2048,1,2,16,64]{4,3,2,1,0:T(8,128)(2,1)} %bitcast_bitcast_fusion) | data formatting | bytes 16777216
  576.4 81.2 %all-to-all-start = ((bf16[16,2,131072]{2,1,0:T(2,128)(2,1)}), bf16[16,2,131072]{2,1,0:T(2,128)(2,1)}, u32[]{:S(2)}, u32[]{:S(2)}) async-start(bf16[16,2,131072]{2,1,0:T(2,128)(2,1)} %reshape.97), calls=%async_computation | async-start | bytes 16777216 | tf_op jit(solution)/shard_map/all_to_all | solution.py:97
  657.6 182.3 %all-to-all-done = bf16[16,2,131072]{2,1,0:T(2,128)(2,1)} async-done(((bf16[16,2,131072]{2,1,0:T(2,128)(2,1)}), bf16[16,2,131072]{2,1,0:T(2,128)(2,1)}, u32[]{:S(2)}, u32[]{:S(2)}) %all-to-all-start) | async-done | bytes 8388640 | tf_op jit(solution)/shard_map/all_to_all | solution.py:97
  839.9 19.2 %reshape.98 = bf16[2048,1,2,16,64]{4,3,2,1,0:T(8,128)(2,1)} reshape(bf16[16,2,131072]{2,1,0:T(2,128)(2,1)} %all-to-all-done) | data formatting | bytes 16777216
  859.1 20.7 %copy.60 = bf16[1,2,16,128,64,16]{3,2,5,4,1,0:T(8,128)(2,1)} copy(bf16[1,2,16,128,64,16]{4,5,1,3,2,0:T(8,128)(2,1)} %bitcast.98) | data formatting | bytes 16777216 | tf_op jit(solution)/shard_map/all_to_all | solution.py:97
  879.8 8.9 copy.48
  888.8 5.5 fusion.70
  897.5 7.3 copy.52
  904.9 5.4 copy.49
  910.3 7.4 copy.51
  917.7 5.5 neg.14
  923.2 32.7 %fusion.57 = f32[128,512,256]{2,1,0:T(8,128)} fusion(bf16[128,256,64]{1,2,0:T(8,128)(2,1)} %neg.14, bf16[128,256,64]{1,2,0:T(8,128)(2,1)} %copy.52, bf16[128,256,64]{1,2,0:T(8,128)(2,1)} %copy.51), kind=kOutput, calls=%fused_computation.72 | convolution fusion | flops 4378853376 | bytes 79691776 | tf_op jit(solution)/shard_map/cif,cjf->cij/dot_general | solution.py:18
  955.9 33.5 %fusion.56 = f32[128,256,256]{2,1,0:T(8,128)} fusion(f32[128,512,256]{2,1,0:T(8,128)} %fusion.57, pred[256,256]{1,0:T(8,128)(4,1)S(1)} %iota_compare_fusion), kind=kLoop, calls=%fused_computation.70 | loop fusion | flops 16777216 | bytes 100728832 | tf_op jit(solution)/shard_map/mul | solution.py:23
  (187 shorter events, 236.5 us)
Async XLA Ops:
  21.5 14.8 %collective-permute-start = (bf16[64,15,4096]{2,0,1:T(8,128)(2,1)}, bf16[64,15,4096]{2,0,1:T(8,128)(2,1)}, u32[]{:S(2)}, u32[]{:S(2)}) collective-permute-start(bf16[64,15,4096]{2,0,1:T(8,128)(2,1)} %copy.61), channel_id=1, source_target_pairs={{0,1},{1,2},{2,3},{4,5},{5,6},{6,7},{8,9},{9,10},{10,11},{12,13},{... | collective-permute-start | bytes 23592968 | tf_op jit(solution)/shard_map/ppermute | solution.py:11
  62.1 4.3 copy-start
  576.4 263.5 %all-to-all-start = ((bf16[16,2,131072]{2,1,0:T(2,128)(2,1)}), bf16[16,2,131072]{2,1,0:T(2,128)(2,1)}, u32[]{:S(2)}, u32[]{:S(2)}) async-start(bf16[16,2,131072]{2,1,0:T(2,128)(2,1)} %reshape.97), calls=%async_computation | async-start | bytes 16777216 | tf_op jit(solution)/shard_map/all_to_all | solution.py:97
where the time goes:
time: 999 us; the launch traced here: 990 us
  other arithmetic  252 us (25%)
  local copies, waits for them, and re-layouts  241 us (24%)
  matrix products  216 us (22%)
  waiting for transfers between devices  195 us (20%)
  starting transfers between devices  82.9 us (8%)
    all_to_all x1, waiting for transfers between devices, per_device(): lax.all_to_all(local_spec[None], ('inp', 'tm', 'pol'), split_axis=2, conc...  182 us
    add x16, other arithmetic, filter_frames(): total + coefficients[tap_index] * block[:, tap_index:tap_index + frame_co...  163 us
    all_to_all x1, starting transfers between devices, per_device(): lax.all_to_all(local_spec[None], ('inp', 'tm', 'pol'), split_axis=2, conc...  81.2 us
    dot_general x16, matrix products, transform(): jnp.einsum('rab,ak->rbk', blocks, table_one, precision=lax.Precision.HIGH...  80.8 us
    unnamed x6, local copies, waits for them, and re-layouts  64.4 us
    reshape x16, local copies, waits for them, and re-layouts, transform(): blocks = filtered.reshape(row_total, inner_len, outer_len)  35.3 us
    mul x1, other arithmetic, correlate(): return packed * (1.0 / total_frames)  33.5 us
    dot_general x1, matrix products, correlate(): jnp.einsum('cif,cjf->cij', stacked, joined, preferred_element_type=jnp.fl...  32.7 us
  transfers between devices with their start and end apart: 2, of which 2 were waited for; matrix products, arithmetic and copies ran while one was open for 0% of the time, Pallas kernels for 0%

commit v1 on v0

--- a/solution.py
+++ b/solution.py
@@ -94,9 +94,11 @@
     n_blocks = lax.axis_size("tm")
     n_halves = lax.axis_size("pol")
     total_frames = frame_count * n_blocks * n_halves
-    arrived = lax.all_to_all(
-        local_spec[None], ("inp", "tm", "pol"), split_axis=2, concat_axis=0, tiled=True
-    )
+    block_2 = local_spec[None]
+    devices_2 = lax.axis_size(("inp", "tm", "pol"))
+    pieces = jnp.stack(jnp.split(block_2, devices_2, axis=2), axis=0)
+    pieces = lax.all_to_all(pieces, ("inp", "tm", "pol"), split_axis=0, concat_axis=0)
+    arrived = jnp.concatenate(pieces, axis=0)
     width = arrived.shape[2]
     arrived = arrived.reshape(n_inputs, n_blocks * n_halves, 2, width, in_dev, frame_count)
     arrived = jnp.transpose(arrived, (2, 3, 0, 4, 1, 5)).reshape(

time: 999 us -> 910 us (0.911)
  local copies, waits for them, and re-layouts: 241 us -> 152 us
    unnamed x6 -> x20, local copies, waits for them, and re-layouts: 64.4 us -> 33.4 us
    all_to_all x2 -> x0, local copies, waits for them, and re-layouts: 29.7 us -> none  [per_device(): lax.all_to_all(local_spec[None], ('inp', 'tm', 'pol'), split_axis=2, conc...]
    while x1 -> x0, local copies, waits for them, and re-layouts: 28.6 us -> none  [per_device(): local_spec = lax.fori_loop(0, in_dev // group_size, one_group, spectra_buf)]
where the time goes in v1:
time: 910 us; the launch traced here: 901 us
  other arithmetic  252 us (28%)
  matrix products  217 us (24%)
  waiting for transfers between devices  195 us (21%)
  local copies, waits for them, and re-layouts  152 us (17%)
  starting transfers between devices  82.9 us (9%)
    all_to_all x1, waiting for transfers between devices, per_device(): lax.all_to_all(pieces, ('inp', 'tm', 'pol'), split_axis=0, concat_axis=0)  182 us
    add x16, other arithmetic, filter_frames(): total + coefficients[tap_index] * block[:, tap_index:tap_index + frame_co...  163 us
    all_to_all x1, starting transfers between devices, per_device(): lax.all_to_all(pieces, ('inp', 'tm', 'pol'), split_axis=0, concat_axis=0)  81.2 us
    dot_general x16, matrix products, transform(): jnp.einsum('rab,ak->rbk', blocks, table_one, precision=lax.Precision.HIGH...  80.8 us
    reshape x16, local copies, waits for them, and re-layouts, transform(): blocks = filtered.reshape(row_total, inner_len, outer_len)  35.2 us
    mul x1, other arithmetic, correlate(): return packed * (1.0 / total_frames)  33.5 us
    unnamed x20, local copies, waits for them, and re-layouts  33.4 us
    dot_general x1, matrix products, correlate(): jnp.einsum('cif,cjf->cij', stacked, joined, preferred_element_type=jnp.fl...  32.8 us
  transfers between devices with their start and end apart: 2, of which 2 were waited for; matrix products, arithmetic and copies ran while one was open for 0% of the time, Pallas kernels for 0%

profile of v1, /device:TPU:11, one launch (start us, length us, event | category | flops | bytes accessed | tf_op | source)
XLA Modules:
  0.0 901.2 jit_solution(10642276049798151621)
XLA Ops:
  0.0 10.5 %slice.391 = bf16[64,15,4096]{2,1,0:T(8,128)(2,1)} slice(bf16[64,16,4096]{2,1,0:T(8,128)(2,1)} %param.4), slice={[0:64], [1:16], [0:4096]} | slice | bytes 15728640 | tf_op jit(solution)/shard_map/slice | solution.py:77
  10.5 11.0 %copy.40 = bf16[64,15,4096]{2,0,1:T(8,128)(2,1)} copy(bf16[64,15,4096]{2,1,0:T(8,128)(2,1)} %slice.391) | data formatting | bytes 15728640
  23.3 13.1 %collective-permute-done = bf16[64,15,4096]{2,0,1:T(8,128)(2,1)} collective-permute-done((bf16[64,15,4096]{2,0,1:T(8,128)(2,1)}, bf16[64,15,4096]{2,0,1:T(8,128)(2,1)}, u32[]{:S(2)}, u32[]{:S(2)}) %collective-permute-start) | collective-permute-done | bytes 7864352 | tf_op jit(solution)/shard_map/ppermute | solution.py:11
  36.3 10.8 %copy.28 = bf16[64,15,4096]{2,1,0:T(8,128)(2,1)} copy(bf16[64,15,4096]{2,0,1:T(8,128)(2,1)} %collective-permute-done) | data formatting | bytes 15728640 | tf_op jit(solution)/shard_map/ppermute | solution.py:11
  47.1 14.9 %pad_maximum_fusion = bf16[64,31,4096]{2,1,0:T(8,128)(2,1)} fusion(bf16[64,16,4096]{2,1,0:T(8,128)(2,1)} %param.4, bf16[64,15,4096]{2,1,0:T(8,128)(2,1)} %copy.28), kind=kLoop, calls=%fused_computation.71 | loop fusion | flops 32505856 | bytes 32505856 | tf_op jit(solution)/shard_map/concatenate | solution.py:78
  62.1 4.3 broadcast_in_dim.31
  66.3 447.3 %while.16 = (s32[]{:T(128)}, bf16[2,2048,64,16]{1,3,2,0:T(8,128)(2,1)}, f32[16,4096]{1,0:T(8,128)S(1)}, bf16[64,31,4096]{2,1,0:T(8,128)(2,1)}, s32[]{:T(128)}, /...) while((s32[]{:T(128)}, ...), condition=%wide.region_1.2_spmd, body=%wide.region_0.1_spmd.sunk | while | flops 822063104 | bytes 40468980 | solution.py:92
  67.1 10.2 %multiply_add_fusion.9 = f32[4,16,4096]{2,1,0:T(8,128)S(1)} fusion(bf16[64,31,4096]{2,1,0:T(8,128)(2,1)} %get-tuple-element.280, s32[]{:T(128)S(6)} %select_n.151, s32[]{:T(128)S(6)} %add.431, s32[]{:T(128)S(6)} %add.432, s32[]{:T(128)S(6)} %add.433, s32[]{:T(128)S(6)} %add.434, s32[]{:T(128)S(6)} %add.435, s32[]{:T(128)S(6)} %add.436, s32[]{:T(128)S(6)} %add.437, ...), kind=kLoop, calls=%fused_computation.8.clone.1 | loop fusion | flops 12320768 | bytes 9699392 | tf_op jit(solution)/shard_map/while/body/eval_jaxpr/add | solution.py:30
  79.5 5.0 fusion.113
  95.0 9.7 %multiply_add_fusion.9 = f32[4,16,4096]{2,1,0:T(8,128)S(1)} fusion(bf16[64,31,4096]{2,1,0:T(8,128)(2,1)} %get-tuple-element.280, s32[]{:T(128)S(6)} %select_n.151, s32[]{:T(128)S(6)} %add.431, s32[]{:T(128)S(6)} %add.432, s32[]{:T(128)S(6)} %add.433, s32[]{:T(128)S(6)} %add.434, s32[]{:T(128)S(6)} %add.435, s32[]{:T(128)S(6)} %add.436, s32[]{:T(128)S(6)} %add.437, ...), kind=kLoop, calls=%fused_computation.8.clone.1 | loop fusion | flops 12320768 | bytes 9699392 | tf_op jit(solution)/shard_map/while/body/eval_jaxpr/add | solution.py:30
  106.8 5.0 fusion.113
  122.4 10.7 %multiply_add_fusion.9 = f32[4,16,4096]{2,1,0:T(8,128)S(1)} fusion(bf16[64,31,4096]{2,1,0:T(8,128)(2,1)} %get-tuple-element.280, s32[]{:T(128)S(6)} %select_n.151, s32[]{:T(128)S(6)} %add.431, s32[]{:T(128)S(6)} %add.432, s32[]{:T(128)S(6)} %add.433, s32[]{:T(128)S(6)} %add.434, s32[]{:T(128)S(6)} %add.435, s32[]{:T(128)S(6)} %add.436, s32[]{:T(128)S(6)} %add.437, ...), kind=kLoop, calls=%fused_computation.8.clone.1 | loop fusion | flops 12320768 | bytes 9699392 | tf_op jit(solution)/shard_map/while/body/eval_jaxpr/add | solution.py:30
  135.3 5.0 fusion.113
  150.8 9.9 %multiply_add_fusion.9 = f32[4,16,4096]{2,1,0:T(8,128)S(1)} fusion(bf16[64,31,4096]{2,1,0:T(8,128)(2,1)} %get-tuple-element.280, s32[]{:T(128)S(6)} %select_n.151, s32[]{:T(128)S(6)} %add.431, s32[]{:T(128)S(6)} %add.432, s32[]{:T(128)S(6)} %add.433, s32[]{:T(128)S(6)} %add.434, s32[]{:T(128)S(6)} %add.435, s32[]{:T(128)S(6)} %add.436, s32[]{:T(128)S(6)} %add.437, ...), kind=kLoop, calls=%fused_computation.8.clone.1 | loop fusion | flops 12320768 | bytes 9699392 | tf_op jit(solution)/shard_map/while/body/eval_jaxpr/add | solution.py:30
  163.0 5.0 fusion.113
  178.5 9.5 %multiply_add_fusion.9 = f32[4,16,4096]{2,1,0:T(8,128)S(1)} fusion(bf16[64,31,4096]{2,1,0:T(8,128)(2,1)} %get-tuple-element.280, s32[]{:T(128)S(6)} %select_n.151, s32[]{:T(128)S(6)} %add.431, s32[]{:T(128)S(6)} %add.432, s32[]{:T(128)S(6)} %add.433, s32[]{:T(128)S(6)} %add.434, s32[]{:T(128)S(6)} %add.435, s32[]{:T(128)S(6)} %add.436, s32[]{:T(128)S(6)} %add.437, ...), kind=kLoop, calls=%fused_computation.8.clone.1 | loop fusion | flops 12320768 | bytes 9699392 | tf_op jit(solution)/shard_map/while/body/eval_jaxpr/add | solution.py:30
  190.2 5.0 fusion.113
  205.7 10.1 %multiply_add_fusion.9 = f32[4,16,4096]{2,1,0:T(8,128)S(1)} fusion(bf16[64,31,4096]{2,1,0:T(8,128)(2,1)} %get-tuple-element.280, s32[]{:T(128)S(6)} %select_n.151, s32[]{:T(128)S(6)} %add.431, s32[]{:T(128)S(6)} %add.432, s32[]{:T(128)S(6)} %add.433, s32[]{:T(128)S(6)} %add.434, s32[]{:T(128)S(6)} %add.435, s32[]{:T(128)S(6)} %add.436, s32[]{:T(128)S(6)} %add.437, ...), kind=kLoop, calls=%fused_computation.8.clone.1 | loop fusion | flops 12320768 | bytes 9699392 | tf_op jit(solution)/shard_map/while/body/eval_jaxpr/add | solution.py:30
  218.0 5.0 fusion.113
  233.6 10.9 %multiply_add_fusion.9 = f32[4,16,4096]{2,1,0:T(8,128)S(1)} fusion(bf16[64,31,4096]{2,1,0:T(8,128)(2,1)} %get-tuple-element.280, s32[]{:T(128)S(6)} %select_n.151, s32[]{:T(128)S(6)} %add.431, s32[]{:T(128)S(6)} %add.432, s32[]{:T(128)S(6)} %add.433, s32[]{:T(128)S(6)} %add.434, s32[]{:T(128)S(6)} %add.435, s32[]{:T(128)S(6)} %add.436, s32[]{:T(128)S(6)} %add.437, ...), kind=kLoop, calls=%fused_computation.8.clone.1 | loop fusion | flops 12320768 | bytes 9699392 | tf_op jit(solution)/shard_map/while/body/eval_jaxpr/add | solution.py:30
  246.7 5.0 fusion.113
  262.2 9.6 %multiply_add_fusion.9 = f32[4,16,4096]{2,1,0:T(8,128)S(1)} fusion(bf16[64,31,4096]{2,1,0:T(8,128)(2,1)} %get-tuple-element.280, s32[]{:T(128)S(6)} %select_n.151, s32[]{:T(128)S(6)} %add.431, s32[]{:T(128)S(6)} %add.432, s32[]{:T(128)S(6)} %add.433, s32[]{:T(128)S(6)} %add.434, s32[]{:T(128)S(6)} %add.435, s32[]{:T(128)S(6)} %add.436, s32[]{:T(128)S(6)} %add.437, ...), kind=kLoop, calls=%fused_computation.8.clone.1 | loop fusion | flops 12320768 | bytes 9699392 | tf_op jit(solution)/shard_map/while/body/eval_jaxpr/add | solution.py:30
  274.0 5.0 fusion.113
  289.5 10.2 %multiply_add_fusion.9 = f32[4,16,4096]{2,1,0:T(8,128)S(1)} fusion(bf16[64,31,4096]{2,1,0:T(8,128)(2,1)} %get-tuple-element.280, s32[]{:T(128)S(6)} %select_n.151, s32[]{:T(128)S(6)} %add.431, s32[]{:T(128)S(6)} %add.432, s32[]{:T(128)S(6)} %add.433, s32[]{:T(128)S(6)} %add.434, s32[]{:T(128)S(6)} %add.435, s32[]{:T(128)S(6)} %add.436, s32[]{:T(128)S(6)} %add.437, ...), kind=kLoop, calls=%fused_computation.8.clone.1 | loop fusion | flops 12320768 | bytes 9699392 | tf_op jit(solution)/shard_map/while/body/eval_jaxpr/add | solution.py:30
  301.9 5.0 fusion.113
  317.4 9.8 %multiply_add_fusion.9 = f32[4,16,4096]{2,1,0:T(8,128)S(1)} fusion(bf16[64,31,4096]{2,1,0:T(8,128)(2,1)} %get-tuple-element.280, s32[]{:T(128)S(6)} %select_n.151, s32[]{:T(128)S(6)} %add.431, s32[]{:T(128)S(6)} %add.432, s32[]{:T(128)S(6)} %add.433, s32[]{:T(128)S(6)} %add.434, s32[]{:T(128)S(6)} %add.435, s32[]{:T(128)S(6)} %add.436, s32[]{:T(128)S(6)} %add.437, ...), kind=kLoop, calls=%fused_computation.8.clone.1 | loop fusion | flops 12320768 | bytes 9699392 | tf_op jit(solution)/shard_map/while/body/eval_jaxpr/add | solution.py:30
  329.5 5.0 fusion.113
  345.0 10.2 %multiply_add_fusion.9 = f32[4,16,4096]{2,1,0:T(8,128)S(1)} fusion(bf16[64,31,4096]{2,1,0:T(8,128)(2,1)} %get-tuple-element.280, s32[]{:T(128)S(6)} %select_n.151, s32[]{:T(128)S(6)} %add.431, s32[]{:T(128)S(6)} %add.432, s32[]{:T(128)S(6)} %add.433, s32[]{:T(128)S(6)} %add.434, s32[]{:T(128)S(6)} %add.435, s32[]{:T(128)S(6)} %add.436, s32[]{:T(128)S(6)} %add.437, ...), kind=kLoop, calls=%fused_computation.8.clone.1 | loop fusion | flops 12320768 | bytes 9699392 | tf_op jit(solution)/shard_map/while/body/eval_jaxpr/add | solution.py:30
  357.4 5.0 fusion.113
  372.9 10.8 %multiply_add_fusion.9 = f32[4,16,4096]{2,1,0:T(8,128)S(1)} fusion(bf16[64,31,4096]{2,1,0:T(8,128)(2,1)} %get-tuple-element.280, s32[]{:T(128)S(6)} %select_n.151, s32[]{:T(128)S(6)} %add.431, s32[]{:T(128)S(6)} %add.432, s32[]{:T(128)S(6)} %add.433, s32[]{:T(128)S(6)} %add.434, s32[]{:T(128)S(6)} %add.435, s32[]{:T(128)S(6)} %add.436, s32[]{:T(128)S(6)} %add.437, ...), kind=kLoop, calls=%fused_computation.8.clone.1 | loop fusion | flops 12320768 | bytes 9699392 | tf_op jit(solution)/shard_map/while/body/eval_jaxpr/add | solution.py:30
  386.0 5.0 fusion.113
  401.5 10.7 %multiply_add_fusion.9 = f32[4,16,4096]{2,1,0:T(8,128)S(1)} fusion(bf16[64,31,4096]{2,1,0:T(8,128)(2,1)} %get-tuple-element.280, s32[]{:T(128)S(6)} %select_n.151, s32[]{:T(128)S(6)} %add.431, s32[]{:T(128)S(6)} %add.432, s32[]{:T(128)S(6)} %add.433, s32[]{:T(128)S(6)} %add.434, s32[]{:T(128)S(6)} %add.435, s32[]{:T(128)S(6)} %add.436, s32[]{:T(128)S(6)} %add.437, ...), kind=kLoop, calls=%fused_computation.8.clone.1 | loop fusion | flops 12320768 | bytes 9699392 | tf_op jit(solution)/shard_map/while/body/eval_jaxpr/add | solution.py:30
  414.5 5.0 fusion.113
  430.0 10.3 %multiply_add_fusion.9 = f32[4,16,4096]{2,1,0:T(8,128)S(1)} fusion(bf16[64,31,4096]{2,1,0:T(8,128)(2,1)} %get-tuple-element.280, s32[]{:T(128)S(6)} %select_n.151, s32[]{:T(128)S(6)} %add.431, s32[]{:T(128)S(6)} %add.432, s32[]{:T(128)S(6)} %add.433, s32[]{:T(128)S(6)} %add.434, s32[]{:T(128)S(6)} %add.435, s32[]{:T(128)S(6)} %add.436, s32[]{:T(128)S(6)} %add.437, ...), kind=kLoop, calls=%fused_computation.8.clone.1 | loop fusion | flops 12320768 | bytes 9699392 | tf_op jit(solution)/shard_map/while/body/eval_jaxpr/add | solution.py:30
  442.5 5.0 fusion.113
  458.0 10.4 %multiply_add_fusion.9 = f32[4,16,4096]{2,1,0:T(8,128)S(1)} fusion(bf16[64,31,4096]{2,1,0:T(8,128)(2,1)} %get-tuple-element.280, s32[]{:T(128)S(6)} %select_n.151, s32[]{:T(128)S(6)} %add.431, s32[]{:T(128)S(6)} %add.432, s32[]{:T(128)S(6)} %add.433, s32[]{:T(128)S(6)} %add.434, s32[]{:T(128)S(6)} %add.435, s32[]{:T(128)S(6)} %add.436, s32[]{:T(128)S(6)} %add.437, ...), kind=kLoop, calls=%fused_computation.8.clone.1 | loop fusion | flops 12320768 | bytes 9699392 | tf_op jit(solution)/shard_map/while/body/eval_jaxpr/add | solution.py:30
  470.6 5.0 fusion.113
  486.1 10.1 %multiply_add_fusion.9 = f32[4,16,4096]{2,1,0:T(8,128)S(1)} fusion(bf16[64,31,4096]{2,1,0:T(8,128)(2,1)} %get-tuple-element.280, s32[]{:T(128)S(6)} %select_n.151, s32[]{:T(128)S(6)} %add.431, s32[]{:T(128)S(6)} %add.432, s32[]{:T(128)S(6)} %add.433, s32[]{:T(128)S(6)} %add.434, s32[]{:T(128)S(6)} %add.435, s32[]{:T(128)S(6)} %add.436, s32[]{:T(128)S(6)} %add.437, ...), kind=kLoop, calls=%fused_computation.8.clone.1 | loop fusion | flops 12320768 | bytes 9699392 | tf_op jit(solution)/shard_map/while/body/eval_jaxpr/add | solution.py:30
  498.4 5.0 fusion.113
  537.0 81.2 %all-to-all-start = ((bf16[16,1,2,128,64,16]{3,5,4,2,1,0:T(8,128)(2,1)}), bf16[16,1,2,128,64,16]{3,5,4,2,1,0:T(8,128)(2,1)}, u32[]{:S(2)}, u32[]{:S(2)}) async-start(bf16[16,1,2,128,64,16]{3,5,4,2,1,0:T(8,128)(2,1)} %fusion.68), calls=%async_computation | async-start | bytes 16777216 | tf_op jit(solution)/shard_map/all_to_all | solution.py:100
  618.2 182.3 %all-to-all-done = bf16[16,1,2,128,64,16]{3,5,4,2,1,0:T(8,128)(2,1)} async-done(((bf16[16,1,2,128,64,16]{3,5,4,2,1,0:T(8,128)(2,1)}), bf16[16,1,2,128,64,16]{3,5,4,2,1,0:T(8,128)(2,1)}, u32[]{:S(2)}, u32[]{:S(2)}) %all-to-all-start) | async-done | bytes 8388640 | tf_op jit(solution)/shard_map/all_to_all | solution.py:100
  800.5 5.5 fusion.86
  809.2 7.4 copy.32
  816.6 5.4 copy.29
  821.9 7.3 copy.31
  829.2 5.5 neg.14
  834.7 32.8 %fusion.57 = f32[128,512,256]{2,1,0:T(8,128)} fusion(bf16[128,256,64]{1,2,0:T(8,128)(2,1)} %neg.14, bf16[128,256,64]{1,2,0:T(8,128)(2,1)} %copy.32, bf16[128,256,64]{1,2,0:T(8,128)(2,1)} %copy.31), kind=kOutput, calls=%fused_computation.72 | convolution fusion | flops 4378853376 | bytes 79691776 | tf_op jit(solution)/shard_map/cif,cjf->cij/dot_general | solution.py:18
  867.5 33.5 %fusion.56 = f32[128,256,256]{2,1,0:T(8,128)} fusion(f32[128,512,256]{2,1,0:T(8,128)} %fusion.57, pred[256,256]{1,0:T(8,128)(4,1)S(1)} %iota_compare_fusion), kind=kLoop, calls=%fused_computation.70 | loop fusion | flops 16777216 | bytes 100728832 | tf_op jit(solution)/shard_map/mul | solution.py:23
  (199 shorter events, 230.2 us)
Async XLA Ops:
  21.5 14.8 %collective-permute-start = (bf16[64,15,4096]{2,0,1:T(8,128)(2,1)}, bf16[64,15,4096]{2,0,1:T(8,128)(2,1)}, u32[]{:S(2)}, u32[]{:S(2)}) collective-permute-start(bf16[64,15,4096]{2,0,1:T(8,128)(2,1)} %copy.40), channel_id=1, source_target_pairs={{0,1},{1,2},{2,3},{4,5},{5,6},{6,7},{8,9},{9,10},{10,11},{12,13},{... | collective-permute-start | bytes 23592968 | tf_op jit(solution)/shard_map/ppermute | solution.py:11
  62.1 4.3 copy-start.1
  513.6 15.8 %copy-start = (bf16[2,2048,64,16]{1,3,2,0:T(8,128)(2,1)S(1)}, bf16[2,2048,64,16]{1,3,2,0:T(8,128)(2,1)}, u32[]{:S(2)}) copy-start(bf16[2,2048,64,16]{1,3,2,0:T(8,128)(2,1)} %get-tuple-element.135) | copy-start | bytes 25165828
  537.0 263.5 %all-to-all-start = ((bf16[16,1,2,128,64,16]{3,5,4,2,1,0:T(8,128)(2,1)}), bf16[16,1,2,128,64,16]{3,5,4,2,1,0:T(8,128)(2,1)}, u32[]{:S(2)}, u32[]{:S(2)}) async-start(bf16[16,1,2,128,64,16]{3,5,4,2,1,0:T(8,128)(2,1)} %fusion.68), calls=%async_computation | async-start | bytes 16777216 | tf_op jit(solution)/shard_map/all_to_all | solution.py:100
